TPU v7x, 32 devices: a whole 2x2x4 slice. The times are simulated.
32 devices in a mesh: layer: 4 (over x, core), latent: 8 (over z, y).
Axes of the slice: x: 2, y: 2, z: 4, core: 2. Of those that a mesh axis runs over, the one named last changes fastest.
Arguments:
- acts: bfloat16 [4, 512, 2048], P('layer', None, 'latent'), may hold values from -6 to 6
- w_enc: bfloat16 [4, 2048, 4096], P('layer', None, 'latent'), may hold values from -0.0625 to 0.0625
- b_enc: float32 [4096], P('latent'), may hold values from -3 to 3
- w_dec: bfloat16 [4, 4096, 2048], P('layer', 'latent'), may hold values from -0.125 to 0.125
- b_dec: bfloat16 [4, 2048], P('layer', 'latent'), may hold values from -3 to 3
Outputs:
- grad_enc: bfloat16 [4, 2048, 4096], P('layer', None, 'latent')
- grad_dec: bfloat16 [4, 4096, 2048], P('layer', 'latent')
- grad_benc: float32 [4096], P('latent')
- grad_bdec: float32 [4, 2048], P('layer', 'latent')
All inputs are finite; a program needn't handle non-finite values.
Results may differ from a plain program's by a relative error of at most 0.014.
Values may be sent and summed in bfloat16 or wider, within the bound.
A program may use at most 64 MiB of HBM per device.

v0:
```python
import jax
import jax.numpy as jnp
from jax import lax
from jax.sharding import PartitionSpec as P


def body(acts, w_enc, b_enc, w_dec, b_dec):
    local = acts[0]
    width_own = local.shape[1]
    enc_own = w_enc[0]
    dec_own = w_dec[0]
    full, bias_full = (
        lax.all_gather(local, "latent", axis=1, tiled=True),
        lax.all_gather(b_dec, "latent", axis=1, tiled=True),
    )
    tokens_all = full.shape[0]
    scale = tokens_all ** (-0.5)
    part = jnp.dot(full, enc_own, preferred_element_type=jnp.float32)
    pre = lax.psum(part, "layer") + b_enc[None, :]
    feat = (jax.nn.softplus(4.0 * pre) / 4.0).astype(jnp.bfloat16)
    rows = tokens_all // lax.axis_size("latent")
    recon = lax.psum_scatter(
        jnp.dot(feat, dec_own, preferred_element_type=jnp.float32),
        "latent",
        scatter_dimension=0,
        tiled=True,
    )
    position = lax.axis_index("latent")
    own_rows = lax.dynamic_slice_in_dim(full, position * rows, rows, 0)
    err_rows = (recon + bias_full.astype(jnp.float32) - own_rows.astype(jnp.float32)).astype(
        jnp.bfloat16
    )
    err = lax.all_gather(err_rows, "latent", axis=0, tiled=True)
    bias_grad_full = scale * jnp.sum(err.astype(jnp.float32), axis=0)
    grad_bdec = lax.dynamic_slice_in_dim(bias_grad_full, position * width_own, width_own, 0)
    dec_prod = lax.dot_general(
        feat, err, (((0,), (0,)), ((), ())), preferred_element_type=jnp.float32
    )
    grad_dec = (scale * dec_prod).astype(jnp.bfloat16)
    feat_term = lax.dot_general(
        err, dec_own, (((1,), (1,)), ((), ())), preferred_element_type=jnp.float32
    )
    grad_feat = scale * lax.psum(feat_term.astype(jnp.bfloat16), "layer").astype(jnp.float32)
    grad_pre = grad_feat * jax.nn.sigmoid(4.0 * pre)
    grad_benc = jnp.sum(grad_pre, axis=0)
    grad_pre_b = grad_pre.astype(jnp.bfloat16)
    enc_prod = lax.dot_general(
        full, grad_pre_b, (((0,), (0,)), ((), ())), preferred_element_type=jnp.float32
    )
    grad_enc = enc_prod.astype(jnp.bfloat16)
    return (grad_enc[None], grad_dec[None], grad_benc, grad_bdec[None])


def solution(mesh):
    return jax.shard_map(
        body,
        mesh=mesh,
        in_specs=(
            P("layer", None, "latent"),
            P("layer", None, "latent"),
            P("latent"),
            P("layer", "latent", None),
            P("layer", "latent"),
        ),
        out_specs=(
            P("layer", None, "latent"),
            P("layer", "latent", None),
            P("latent"),
            P("layer", "latent"),
        ),
        check_vma=False,
    )
```

profile of v0, /device:TPU:0, one launch (start us, length us, event | category | flops | bytes accessed | tf_op | source)
XLA Modules:
  0.0 300.1 jit_solution(7235428167630968773)
XLA Ops:
  7.2 0.0 copy-start
  7.2 0.0 all-gather.6.cloned.1.call-start
  7.2 0.7 all-gather.6.cloned.1.call-update
  7.9 0.0 copy-start.2
  7.9 0.0 all-reduce.3.cloned.1.call-start
  8.0 55.2 %all-gather.6.cloned.1.call-done = bf16[1,512,2048]{2,1,0:T(8,128)(2,1)} async-done(((bf16[1,512,256]{2,1,0:T(8,128)(2,1)}), bf16[1,512,2048]{2,1,0:T(8,128)(2,1)}) %all-gather.6.cloned.1.call-update) | async-done | bytes 2097168 | tf_op jit(solution)/shard_map/all_gather | solution.py:13
  63.1 4.4 %fusion.6 = f32[512,512]{1,0:T(8,128)} fusion(bf16[1,2048,512]{2,1,0:T(8,128)(2,1)} %param.6, bf16[1,512,2048]{2,1,0:T(8,128)(2,1)} %all-gather.6.cloned.1.call-done), kind=kOutput, calls=%fused_computation.10 | convolution fusion | flops 1073741824 | bytes 5242880 | tf_op jit(solution)/shard_map/dot_general | solution.py:18
  67.6 0.0 all-reduce.3.cloned.1.call-update
  67.6 0.0 reduce-scatter.2.cloned.1.call-start
  67.7 34.6 %all-reduce.3.cloned.1.call-done = f32[512,512]{1,0:T(8,128)} async-done(((f32[512,512]{1,0:T(8,128)}), f32[512,512]{1,0:T(8,128)}) %all-reduce.3.cloned.1.call-update) | async-done | bytes 1048592 | tf_op jit(solution)/shard_map/psum | solution.py:19
  102.2 0.0 copy-done
  102.2 0.0 copy-done.2
  102.2 4.9 %fusion.4 = f32[512,2048]{1,0:T(8,128)} fusion(bf16[1,512,2048]{2,1,0:T(8,128)(2,1)S(1)} %copy-done, f32[512,512]{1,0:T(8,128)} %all-reduce.3.cloned.1.call-done, f32[512]{0:T(512)S(1)} %copy-done.2), kind=kOutput, calls=%fused_computation.8 | convolution fusion | flops 1076363264 | bytes 7342080 | tf_op jit(solution)/shard_map/dot_general | solution.py:23
  107.1 0.0 reduce-scatter.2.cloned.1.call-update
  107.2 0.0 all-gather.4.cloned.1.call-start
  107.2 0.6 copy-done.3
  107.8 20.7 %all_gather.10 = bf16[1,2048]{1,0:T(2,128)(2,1)S(1)} all-gather(bf16[1,256]{1,0:T(2,128)(2,1)S(1)} %copy-done.3), channel_id=1, replica_groups=mesh['layer'=4,'latent'=8] {'latent'}, dimensions={1}, use_global_device_ids=true | all-gather | bytes 4608 | tf_op jit(solution)/shard_map/all_gather | solution.py:14
  128.5 67.6 %reduce-scatter.2.cloned.1.call-done = f32[64,2048]{1,0:T(8,128)} async-done(((f32[512,2048]{1,0:T(8,128)}), f32[64,2048]{1,0:T(8,128)}) %reduce-scatter.2.cloned.1.call-update) | async-done | bytes 524304 | tf_op jit(solution)/shard_map/reduce_scatter | solution.py:22
  196.1 1.9 fusion.15
  198.0 0.0 all-gather.4.cloned.1.call-update
  198.0 0.0 all-reduce.5.cloned.1.call-start
  198.1 49.4 %all-gather.4.cloned.1.call-done = bf16[512,2048]{1,0:T(8,128)(2,1)} async-done(((bf16[64,2048]{1,0:T(8,128)(2,1)}), bf16[512,2048]{1,0:T(8,128)(2,1)}) %all-gather.4.cloned.1.call-update) | async-done | bytes 2097168 | tf_op jit(solution)/shard_map/all_gather | solution.py:33
  247.5 3.7 %fusion.10 = bf16[512,512]{1,0:T(8,128)(2,1)} fusion(bf16[512,2048]{1,0:T(8,128)(2,1)} %all-gather.4.cloned.1.call-done, bf16[1,512,2048]{2,1,0:T(8,128)(2,1)S(1)} %copy-done), kind=kOutput, calls=%fused_computation.14 | convolution fusion | flops 1074003968 | bytes 4718592 | tf_op jit(solution)/shard_map/dot_general | solution.py:40
  251.1 0.0 all-reduce.5.cloned.1.call-update
  251.1 2.0 convert_reduce_fusion
  253.2 0.6 dynamic-slice_multiply_fusion
  253.8 0.0 copy-done.1
  253.8 4.8 %fusion.1 = bf16[1,512,2048]{2,1,0:T(8,128)(2,1)} fusion(bf16[512,2048]{1,0:T(8,128)(2,1)} %all-gather.4.cloned.1.call-done, f32[512,512]{1,0:T(8,128)S(1)} %copy-done.1, f32[512]{0:T(512)S(1)} %copy-done.2), kind=kOutput, calls=%fused_computation.5 | convolution fusion | flops 1078460416 | bytes 5244928 | tf_op jit(solution)/shard_map/dot_general | solution.py:36
  258.6 24.6 %all-reduce.5.cloned.1.call-done = bf16[512,512]{1,0:T(8,128)(2,1)} async-done(((bf16[512,512]{1,0:T(8,128)(2,1)}), bf16[512,512]{1,0:T(8,128)(2,1)}) %all-reduce.5.cloned.1.call-update) | async-done | bytes 524304 | tf_op jit(solution)/shard_map/psum | solution.py:43
  283.2 4.5 %fusion = bf16[1,2048,512]{1,2,0:T(8,128)(2,1)} fusion(bf16[1,512,2048]{2,1,0:T(8,128)(2,1)} %all-gather.6.cloned.1.call-done, bf16[512,512]{1,0:T(8,128)(2,1)} %all-reduce.5.cloned.1.call-done, f32[512,512]{1,0:T(8,128)S(1)} %copy-done.1, f32[512]{0:T(512)S(1)} %copy-done.2), kind=kOutput, calls=%fused_computation.4 | convolution fusion | flops 1077149696 | bytes 5769216 | tf_op jit(solution)/shard_map/dot_general | solution.py:47
  287.7 3.9 %copy.9 = bf16[1,2048,512]{2,1,0:T(8,128)(2,1)} copy(bf16[1,2048,512]{1,2,0:T(8,128)(2,1)} %fusion) | data formatting | bytes 4194304
  291.6 2.0 fusion.17
  (3 shorter events, 0.0 us)
Async XLA Ops:
  7.2 95.1 %copy-start = (bf16[1,512,2048]{2,1,0:T(8,128)(2,1)S(1)}, bf16[1,512,2048]{2,1,0:T(8,128)(2,1)}, u32[]{:S(2)}) copy-start(bf16[1,512,2048]{2,1,0:T(8,128)(2,1)} %param.8) | copy-start | bytes 6291460
  7.2 56.0 %all-gather.6.cloned.1.call-start = ((), (), s32[]{:S(2)}) async-start(), calls=%async_computation.5 | async-start | bytes 2359296 | tf_op jit(solution)/shard_map/all_gather | solution.py:13
  7.9 94.3 %copy-start.2 = (f32[512]{0:T(512)S(1)}, f32[512]{0:T(512)}, u32[]{:S(2)}) copy-start(f32[512]{0:T(512)} %param.7) | copy-start | bytes 6148
  7.9 94.3 %all-reduce.3.cloned.1.call-start = ((), (), s32[]{:S(2)}) async-start(), calls=%async_computation.1 | async-start | bytes 2097152 | tf_op jit(solution)/shard_map/psum | solution.py:19
  67.6 128.5 %reduce-scatter.2.cloned.1.call-start = ((), (), s32[]{:S(2)}) async-start(), calls=%async_computation.2 | async-start | bytes 4718592 | tf_op jit(solution)/shard_map/reduce_scatter | solution.py:22
  107.1 0.7 copy-start.3
  107.2 140.3 %all-gather.4.cloned.1.call-start = ((), (), s32[]{:S(2)}) async-start(), calls=%async_computation.3 | async-start | bytes 2359296 | tf_op jit(solution)/shard_map/all_gather | solution.py:33
  198.0 85.2 %all-reduce.5.cloned.1.call-start = ((), (), s32[]{:S(2)}) async-start(), calls=%async_computation.4 | async-start | bytes 1048576 | tf_op jit(solution)/shard_map/psum | solution.py:43
  251.1 2.7 copy-start.1
Sparse Core Ops, SparseCore 0:
  10.0 53.0 all-gather.5
  67.7 34.4 all-reduce.2
  107.3 88.7 reduce-scatter.1
  198.7 48.7 all-gather.3
  251.3 31.9 all-reduce.4
where the time goes:
time: 301 us; the launch traced here: 300 us
  waiting for transfers between devices  232 us (77%)
  matrix products  22.3 us (7%)
  blocking collectives  20.7 us (7%)
  between operations  13.8 us (5%)
  other arithmetic  6.54 us (2%)
  local copies, waits for them, and re-layouts  4.53 us (2%)
    reduce_scatter x1, waiting for transfers between devices, body(): lax.psum_scatter(jnp.dot(feat, dec_own, preferred_element_type=jnp.float3...  67.6 us
    all_gather x1, waiting for transfers between devices, body(): lax.all_gather(local, 'latent', axis=1, tiled=True)  55.2 us
    all_gather x1, waiting for transfers between devices, body(): err = lax.all_gather(err_rows, 'latent', axis=0, tiled=True)  49.4 us
    psum x1, waiting for transfers between devices, body(): pre = lax.psum(part, 'layer') + b_enc[None, :]  34.6 us
    psum x1, waiting for transfers between devices, body(): lax.psum(feat_term.astype(jnp.bfloat16), 'layer').astype(jnp.float32)  24.6 us
    all_gather x1, blocking collectives, body(): lax.all_gather(b_dec, 'latent', axis=1, tiled=True)  20.7 us
  transfers between devices with their start and end apart: 5, of which 5 were waited for; matrix products, arithmetic and copies ran while one was open for 3% of the time, Pallas kernels for 0%

commit v1 on v0

v1 whole, which is shorter than its diff:
```python
import functools

import jax
import jax.numpy as jnp
from jax import lax
from jax.experimental import pallas as pl
from jax.experimental.pallas import tpu as pltpu
from jax.sharding import PartitionSpec as P

MESH = pl.DeviceIdType.MESH
F32 = jnp.float32
BF16 = jnp.bfloat16
INNER = 2


def place(n):
    me = lax.axis_index("latent")
    return me // INNER, lax.rem(me, INNER), n // INNER


def greet(n):
    z, y, depth = place(n)
    barrier = pltpu.get_barrier_semaphore()

    def signal(index):
        pl.semaphore_signal(barrier, inc=1, device_id={"latent": index}, device_id_type=MESH)

    signal(z * INNER + 1 - y)

    @pl.when(z > 0)
    def _():
        signal((z - 1) * INNER + y)

    @pl.when(z < depth - 1)
    def _():
        signal((z + 1) * INNER + y)

    peers = 1 + jnp.where(z > 0, 1, 0) + jnp.where(z < depth - 1, 1, 0)
    pl.semaphore_wait(barrier, peers)


def remote(src, dst, send, recv, index, axis="latent"):
    return pltpu.make_async_remote_copy(
        src_ref=src,
        dst_ref=dst,
        send_sem=send,
        recv_sem=recv,
        device_id={axis: index},
        device_id_type=MESH,
    )


def gather_kernel(n, view_in, view, x_ref, out_ref, local_sem, send, recv):
    z, y, depth = place(n)
    greet(n)
    me = z * INNER + y
    partner = z * INNER + 1 - y

    def move(h, block, way, own, start):
        src = view_in(x_ref, h) if own else view(out_ref, block, h)
        target = (partner, me + INNER, me - INNER)[way]
        copy = remote(src, view(out_ref, block, h), send.at[way, h, block], recv.at[h, block], target)
        if start:
            copy.start()
        else:
            copy.wait_send()

    def along(h, block, own, start, up=True, down=True):
        if up:

            @pl.when(z < depth - 1)
            def _():
                move(h, block, 1, own, start)

        if down:

            @pl.when(z > 0)
            def _():
                move(h, block, 2, own, start)

    def arrive(h, block):
        spot = view(out_ref, block, h)
        remote(spot, spot, send.at[0, h, block], recv.at[h, block], partner).wait_recv()

    def run(start):
        move(1, me, 0, True, start)
        along(0, me, True, start)
        along(1, me, True, start)
        move(0, me, 0, True, start)
        if start:
            keep = [
                pltpu.make_async_copy(view_in(x_ref, h), view(out_ref, me, h), local_sem.at[h])
                for h in range(2)
            ]
            for copy in keep:
                copy.start()
            arrive(1, partner)
        along(1, partner, False, start)
        for d in range(1, depth):
            for below in (True, False):
                at = z - d if below else z + d

                @pl.when(at >= 0 if below else at < depth)
                def _():
                    for h, side in ((0, y), (1, y), (1, 1 - y)):
                        block = at * INNER + side
                        if start:
                            arrive(h, block)
                        along(h, block, False, start, up=below, down=not below)
                        if h == 0:
                            move(0, block, 0, False, start)

        if start:
            for copy in keep:
                copy.wait()
            for at in range(depth):
                arrive(0, at * INNER + 1 - y)

    run(True)
    run(False)


def gather_blocks(x, n, by_rows, collective_id):
    rows, width = x.shape
    if by_rows:
        shape, half = (n * rows, width), width // 2
        flat = rows % 16 == 0 and half % 128 == 0
        blocks = (rows, half)
        view_in = lambda ref, h: ref.at[:, pl.ds(h * half, half)]
        view = lambda ref, j, h: ref.at[
            pl.ds(pl.multiple_of(j * rows, rows), rows), pl.ds(h * half, half)
        ]
    else:
        shape, half = (rows, n * width), rows // 2
        flat = width % 128 == 0 and half % 16 == 0
        blocks = (half, width)
        view_in = lambda ref, h: ref.at[pl.ds(h * half, half), :]
        view = lambda ref, j, h: ref.at[
            pl.ds(h * half, half), pl.ds(pl.multiple_of(j * width, width), width)
        ]
    if not flat:
        if by_rows:
            x = x.reshape(rows, 2, half).transpose(1, 0, 2)
        else:
            x = x.reshape(2, half, width)
        shape = (n, 2) + blocks
        view_in = lambda ref, h: ref.at[h]
        view = lambda ref, j, h: ref.at[j, h]
    out = pl.pallas_call(
        functools.partial(gather_kernel, n, view_in, view),
        out_shape=jax.ShapeDtypeStruct(shape, x.dtype),
        in_specs=[pl.BlockSpec(memory_space=pltpu.VMEM)],
        out_specs=pl.BlockSpec(memory_space=pltpu.VMEM),
        scratch_shapes=[
            pltpu.SemaphoreType.DMA((2,)),
            pltpu.SemaphoreType.DMA((3, 2, n)),
            pltpu.SemaphoreType.DMA((2, n)),
        ],
        compiler_params=pltpu.CompilerParams(collective_id=collective_id, has_side_effects=True),
        name="gather_rows" if by_rows else "gather_columns",
    )(x)
    if flat:
        return out
    if by_rows:
        return out.transpose(0, 2, 1, 3).reshape(n * rows, width)
    return out.transpose(1, 2, 0, 3).reshape(rows, n * width)


def scatter_kernel(
    n, view, part, out_ref, side_in, up_in, down_in, up_out, down_out, last_in, last_out,
    side_sem, up_sem, down_sem, last_sem,
):
    z, y, depth = place(n)
    greet(n)
    me = z * INNER + y
    partner = z * INNER + 1 - y

    def side_copy(at):
        return remote(
            view(part, at * INNER + 1 - y, 0), side_in.at[at],
            side_sem.at[0, at], side_sem.at[1, at], partner,
        )

    def line_copy(up, lane, at):
        stay, land, sems = (up_out, up_in, up_sem) if up else (down_out, down_in, down_sem)
        return remote(
            stay.at[lane, at], land.at[lane, at], sems.at[0, lane, at], sems.at[1, lane, at],
            me + INNER if up else me - INNER,
        )

    last_copy = remote(last_out, last_in, last_sem.at[0], last_sem.at[1], partner)

    for at in range(depth):
        side_copy(at).start()

    def own_term(lane, at):
        if lane < 2:
            return view(part, at * INNER + lane, 1)[...].astype(F32)
        return view(part, at * INNER + y, 0)[...].astype(F32) + side_in[at].astype(F32)

    for d in range(depth - 1, 0, -1):
        for lane in range(3):
            if lane == 2:
                for up in (True, False):
                    at = z + d if up else z - d

                    @pl.when(at < depth if up else at >= 0)
                    def _():
                        side_copy(at).wait_recv()

            for up in (True, False):
                at = z + d if up else z - d
                valid = at < depth if up else at >= 0
                inner = z > 0 if up else z < depth - 1
                stay, land = (up_out, up_in) if up else (down_out, down_in)

                @pl.when(jnp.logical_and(valid, inner))
                def _():
                    line_copy(up, lane, at).wait_recv()
                    stay[lane, at] = (own_term(lane, at) + land[lane, at].astype(F32)).astype(BF16)

                @pl.when(jnp.logical_and(valid, jnp.logical_not(inner)))
                def _():
                    stay[lane, at] = own_term(lane, at).astype(BF16)

                @pl.when(valid)
                def _():
                    line_copy(up, lane, at).start()

    side_copy(z).wait_recv()

    @pl.when(z > 0)
    def _():
        for lane in range(3):
            line_copy(True, lane, z).wait_recv()

    @pl.when(z == 0)
    def _():
        for lane in range(3):
            up_in[lane, z] = jnp.zeros(up_in.shape[2:], BF16)

    @pl.when(z < depth - 1)
    def _():
        for lane in range(3):
            line_copy(False, lane, z).wait_recv()

    @pl.when(z == depth - 1)
    def _():
        for lane in range(3):
            down_in[lane, z] = jnp.zeros(down_in.shape[2:], BF16)

    def both(lane):
        return up_in[lane, z].astype(F32) + down_in[lane, z].astype(F32)

    other = 1 - y
    last_out[...] = (view(part, partner, 1)[...].astype(F32) + both(other)).astype(BF16)
    last_copy.start()
    out_ref[0] = own_term(2, z) + both(2)
    last_copy.wait_recv()
    out_ref[1] = view(part, me, 1)[...].astype(F32) + both(y) + last_in[...].astype(F32)
    last_copy.wait_send()
    for at in range(depth):
        side_copy(at).wait_send()
    for d in range(depth - 1, 0, -1):
        for up in (True, False):
            at = z + d if up else z - d

            @pl.when(at < depth if up else at >= 0)
            def _():
                for lane in range(3):
                    line_copy(up, lane, at).wait_send()


def scatter_sum(x, n, collective_id):
    tokens, width = x.shape
    rows, half, depth = tokens // n, width // 2, n // INNER
    flat = rows % 16 == 0 and half % 128 == 0
    if flat:
        view = lambda ref, j, h: ref.at[
            pl.ds(pl.multiple_of(j * rows, rows), rows), pl.ds(h * half, half)
        ]
    else:
        x = x.reshape(n, rows, 2, half).transpose(0, 2, 1, 3)
        view = lambda ref, j, h: ref.at[j, h]
    line = pltpu.VMEM((3, depth, rows, half), BF16)
    out = pl.pallas_call(
        functools.partial(scatter_kernel, n, view),
        out_shape=jax.ShapeDtypeStruct((2, rows, half), F32),
        in_specs=[pl.BlockSpec(memory_space=pltpu.VMEM)],
        out_specs=pl.BlockSpec(memory_space=pltpu.VMEM),
        scratch_shapes=[
            pltpu.VMEM((depth, rows, half), BF16),
            line, line, line, line,
            pltpu.VMEM((rows, half), BF16),
            pltpu.VMEM((rows, half), BF16),
            pltpu.SemaphoreType.DMA((2, depth)),
            pltpu.SemaphoreType.DMA((2, 3, depth)),
            pltpu.SemaphoreType.DMA((2, 3, depth)),
            pltpu.SemaphoreType.DMA((2,)),
        ],
        compiler_params=pltpu.CompilerParams(collective_id=collective_id, has_side_effects=True),
        name="scatter_sum",
    )(x)
    return jnp.concatenate([out[0], out[1]], axis=1)


def reduce_kernel(part, out_ref, pair_in, far_in, far_out, sems):
    place_own = lax.axis_index("layer")
    core = lax.rem(place_own, 2)
    pair = place_own + 1 - 2 * core
    far = lax.rem(place_own + 2, 4)
    barrier = pltpu.get_barrier_semaphore()
    for index in (pair, far):
        pl.semaphore_signal(barrier, inc=1, device_id={"layer": index}, device_id_type=MESH)
    pl.semaphore_wait(barrier, 2)
    first = remote(part.at[1 - core], pair_in, sems.at[0], sems.at[1], pair, "layer")
    first.start()
    first.wait_recv()
    far_out[...] = (part[core].astype(F32) + pair_in[...].astype(F32)).astype(BF16)
    second = remote(far_out, far_in, sems.at[2], sems.at[3], far, "layer")
    second.start()
    second.wait_recv()
    out_ref[core] = (far_out[...].astype(F32) + far_in[...].astype(F32)).astype(BF16)
    third = remote(out_ref.at[core], out_ref.at[core], sems.at[4], sems.at[5], pair, "layer")
    third.start()
    third.wait_recv()
    first.wait_send()
    second.wait_send()
    third.wait_send()


def layer_sum(x, collective_id):
    tokens, width = x.shape
    half = tokens // 2
    out = pl.pallas_call(
        reduce_kernel,
        out_shape=jax.ShapeDtypeStruct((2, half, width), BF16),
        in_specs=[pl.BlockSpec(memory_space=pltpu.VMEM)],
        out_specs=pl.BlockSpec(memory_space=pltpu.VMEM),
        scratch_shapes=[pltpu.VMEM((half, width), BF16)] * 3 + [pltpu.SemaphoreType.DMA((6,))],
        compiler_params=pltpu.CompilerParams(collective_id=collective_id, has_side_effects=True),
        name="layer_sum",
    )(x.reshape(2, half, width))
    return out.reshape(tokens, width).astype(F32)


def body(n, acts, w_enc, b_enc, w_dec, b_dec):
    local = acts[0]
    width_own = local.shape[1]
    enc_own = w_enc[0]
    dec_own = w_dec[0]
    full = gather_blocks(local, n, False, 0)
    tokens_all = full.shape[0]
    scale = tokens_all ** (-0.5)
    position = lax.axis_index("latent")
    rows = tokens_all // n
    part = jnp.dot(full, enc_own, preferred_element_type=F32).astype(BF16)
    pre = layer_sum(part, 1) + b_enc[None, :]
    feat = (jax.nn.softplus(4.0 * pre) / 4.0).astype(BF16)
    bias_own = lax.dynamic_update_slice(
        jnp.zeros((1, n * width_own), F32), b_dec.astype(F32), (0, position * width_own)
    )
    term = jnp.dot(feat, dec_own, preferred_element_type=F32) + bias_own
    recon = scatter_sum(term.astype(BF16), n, 2)
    own_rows = lax.dynamic_slice_in_dim(full, position * rows, rows, 0)
    err_rows = (recon - own_rows.astype(F32)).astype(BF16)
    err = gather_blocks(err_rows, n, True, 3)
    bias_grad_full = scale * jnp.sum(err.astype(F32), axis=0)
    grad_bdec = lax.dynamic_slice_in_dim(bias_grad_full, position * width_own, width_own, 0)
    dec_prod = lax.dot_general(
        feat, err, (((0,), (0,)), ((), ())), preferred_element_type=F32
    )
    grad_dec = (scale * dec_prod).astype(BF16)
    feat_term = lax.dot_general(
        err, dec_own, (((1,), (1,)), ((), ())), preferred_element_type=F32
    )
    grad_feat = scale * layer_sum(feat_term.astype(BF16), 4)
    grad_pre = grad_feat * jax.nn.sigmoid(4.0 * pre)
    grad_benc = jnp.sum(grad_pre, axis=0)
    grad_pre_b = grad_pre.astype(BF16)
    enc_prod = lax.dot_general(
        full, grad_pre_b, (((0,), (0,)), ((), ())), preferred_element_type=F32
    )
    grad_enc = enc_prod.astype(BF16)
    return (grad_enc[None], grad_dec[None], grad_benc, grad_bdec[None])


def solution(mesh):
    return jax.shard_map(
        functools.partial(body, mesh.shape["latent"]),
        mesh=mesh,
        in_specs=(
            P("layer", None, "latent"),
            P("layer", None, "latent"),
            P("latent"),
            P("layer", "latent", None),
            P("layer", "latent"),
        ),
        out_specs=(
            P("layer", None, "latent"),
            P("layer", "latent", None),
            P("latent"),
            P("layer", "latent"),
        ),
        check_vma=False,
    )
```

time: 301 us -> 164 us (0.54)
  waiting for transfers between devices: 232 us -> 0 us
  Pallas kernels: 0 us -> 132 us
  blocking collectives: 20.7 us -> 0 us
  between operations: 13.8 us -> 0.77 us
  matrix products: 22.3 us -> 17.5 us
    pallas_call x0 -> x5, Pallas kernels: none -> 132 us  [the longest x2 68.1 us: gather_blocks(): pl.pallas_call(functools.partial(gather_kernel, n, view_in, view), out_sh...]
    all_gather x2 -> x0, waiting for transfers between devices: 105 us -> none  [the longest x1 55.2 us: body(): lax.all_gather(local, 'latent', axis=1, tiled=True)]
    reduce_scatter x1 -> x0, waiting for transfers between devices: 67.6 us -> none  [body(): lax.psum_scatter(jnp.dot(feat, dec_own, preferred_element_type=jnp.float3...]
    psum x2 -> x0, waiting for transfers between devices: 59.2 us -> none  [the longest x1 34.6 us: body(): pre = lax.psum(part, 'layer') + b_enc[None, :]]
    all_gather x1 -> x0, blocking collectives: 20.7 us -> none  [body(): lax.all_gather(b_dec, 'latent', axis=1, tiled=True)]
  transfers between devices with their start and end apart: 5 -> 0, of which waited for: 5 -> 0; matrix products, arithmetic and copies ran while one was open for 3% -> 0% of each run, Pallas kernels for 0% -> 0%
where the time goes in v1:
time: 164 us
  Pallas kernels  132 us (80%)
  matrix products  17.5 us (11%)
  other arithmetic  7.63 us (5%)
  local copies, waits for them, and re-layouts  5.3 us (3%)
    pallas_call x2, Pallas kernels, gather_blocks(): pl.pallas_call(functools.partial(gather_kernel, n, view_in, view), out_sh...  68.1 us
    pallas_call x1, Pallas kernels, scatter_sum(): pl.pallas_call(functools.partial(scatter_kernel, n, view), out_shape=jax....  39.1 us
    pallas_call x2, Pallas kernels, layer_sum(): pl.pallas_call(reduce_kernel, out_shape=jax.ShapeDtypeStruct((2, half, wi...  25.3 us
    dot_general x1, matrix products, body(): lax.dot_general(feat, err, (((0,), (0,)), ((), ())), preferred_element_ty...  4.34 us
    dot_general x1, matrix products, body(): part = jnp.dot(full, enc_own, preferred_element_type=F32).astype(BF16)  4.27 us
    unnamed x13, local copies, waits for them, and re-layouts  3.95 us
    dot_general x1, matrix products, body(): lax.dot_general(err, dec_own, (((1,), (1,)), ((), ())), preferred_element...  3.72 us

profile of v1, /device:TPU:0, one launch (start us, length us, event | category | flops | bytes accessed | tf_op | source)
XLA Modules:
  0.0 163.7 jit_solution(545478676106481197)
XLA Ops:
  0.6 0.0 copy-start
  0.6 34.2 %gather_columns.1 = bf16[512,2048]{1,0:T(8,128)(2,1)} custom-call(bf16[512,256]{1,0:T(8,128)(2,1)} %bitcast.50), custom_call_target="tpu_custom_call" | custom-call | tf_op jit(solution)/shard_map/gather_columns/pallas_call | solution.py:149
  34.8 0.0 copy-start.4
  34.8 4.3 %fusion.7 = bf16[512,512]{1,0:T(8,128)(2,1)} fusion(bf16[512,2048]{1,0:T(8,128)(2,1)} %gather_columns.1, bf16[1,2048,512]{2,1,0:T(8,128)(2,1)} %param.6), kind=kOutput, calls=%fused_computation.13 | convolution fusion | flops 1074003968 | bytes 4718592 | tf_op jit(solution)/shard_map/dot_general | solution.py:357
  39.1 0.0 copy-start.5
  39.1 13.2 %layer_sum.2 = bf16[2,256,512]{2,1,0:T(8,128)(2,1)} custom-call(bf16[2,256,512]{2,1,0:T(8,128)(2,1)} %bitcast.48), custom_call_target="tpu_custom_call" | custom-call | tf_op jit(solution)/shard_map/layer_sum/pallas_call | solution.py:335
  52.4 0.0 copy-done.4
  52.4 1.8 %fusion.14 = bf16[2,256,512]{2,1,0:T(8,128)(2,1)S(1)} fusion(bf16[2,256,512]{2,1,0:T(8,128)(2,1)} %layer_sum.2, f32[512]{0:T(512)S(1)} %copy-done.4), kind=kLoop, calls=%fused_computation.16 | loop fusion | flops 2883584 | bytes 1050624 | tf_op jit(solution)/shard_map/convert_element_type | solution.py:359
  54.1 0.0 copy-done.5
  54.2 0.3 dynamic_update_slice.4
  54.5 0.0 copy-done
  54.5 2.6 %add_convert_fusion.part = bf16[512,2048]{1,0:T(8,128)(2,1)} fusion(bf16[512,512]{1,0:T(8,128)(2,1)S(1)} %bitcast.47, bf16[1,512,2048]{2,1,0:T(8,128)(2,1)S(1)} %copy-done, f32[2048]{0:T(1024)S(1)} %dynamic_update_slice.4), kind=kOutput, calls=%fused_computation.2 | convolution fusion | flops 1075838976 | bytes 4726784 | tf_op jit(solution)/shard_map/dot_general | solution.py:363
  57.0 39.1 %scatter_sum.1 = f32[2,64,1024]{2,1,0:T(8,128)} custom-call(bf16[512,2048]{1,0:T(8,128)(2,1)} %add_convert_fusion.part), custom_call_target="tpu_custom_call" | custom-call | tf_op jit(solution)/shard_map/scatter_sum/pallas_call | solution.py:286
  96.2 1.1 slice_bitcast_fusion.1
  97.2 1.7 %fusion.19.x_ref = bf16[64,2048]{1,0:T(8,128)(2,1)} fusion(f32[64,1024]{1,0:T(8,128)S(1)} %get-tuple-element.13, f32[64,1024]{1,0:T(8,128)S(1)} %get-tuple-element.12, bf16[512,2048]{1,0:T(8,128)(2,1)} %gather_columns.1, s32[]{:T(128)S(6)} %select_n.16), kind=kLoop, calls=%fused_computation.27 | loop fusion | flops 524288 | bytes 1048580 | tf_op jit(solution)/shard_map/convert_element_type | solution.py:366
  98.9 33.9 %gather_rows.1 = bf16[512,2048]{1,0:T(8,128)(2,1)} custom-call(bf16[64,2048]{1,0:T(8,128)(2,1)} %fusion.19.x_ref), custom_call_target="tpu_custom_call" | custom-call | tf_op jit(solution)/shard_map/gather_rows/pallas_call | solution.py:149
  132.8 0.0 copy-start.2
  132.9 3.7 %fusion.10 = bf16[512,512]{1,0:T(8,128)(2,1)} fusion(bf16[512,2048]{1,0:T(8,128)(2,1)} %gather_rows.1, bf16[1,512,2048]{2,1,0:T(8,128)(2,1)S(1)} %copy-done), kind=kOutput, calls=%fused_computation.14 | convolution fusion | flops 1074003968 | bytes 4718592 | tf_op jit(solution)/shard_map/dot_general | solution.py:374
  136.6 12.1 %layer_sum.3 = bf16[2,256,512]{2,1,0:T(8,128)(2,1)} custom-call(bf16[2,256,512]{2,1,0:T(8,128)(2,1)} %bitcast.49), custom_call_target="tpu_custom_call" | custom-call | tf_op jit(solution)/shard_map/layer_sum/pallas_call | solution.py:335
  148.7 0.0 copy-done.2
  148.7 0.0 copy-start.3
  148.7 2.2 %multiply_reduce_fusion = (f32[512]{0:T(512)}, f32[2,256,512]{2,1,0:T(8,128)S(1)}) fusion(bf16[2,256,512]{2,1,0:T(8,128)(2,1)S(1)} %copy-done.2, f32[512]{0:T(512)S(1)} %copy-done.4, bf16[2,256,512]{2,1,0:T(8,128)(2,1)} %layer_sum.3), kind=kLoop, calls=%fused_computation.23 | loop fusion | flops 2620928 | bytes 2101248 | tf_op jit(solution)/shard_map/reduce_sum | solution.py:379
  150.8 1.0 fusion.16
  151.8 0.0 copy-done.3
  151.8 2.6 %fusion = bf16[1,2048,512]{1,2,0:T(8,128)(2,1)} fusion(bf16[512,512]{1,0:T(8,128)(2,1)S(1)} %get-tuple-element.9, bf16[512,2048]{1,0:T(8,128)(2,1)S(1)} %copy-done.3), kind=kOutput, calls=%fused_computation.6 | convolution fusion | flops 1074790400 | bytes 4718592 | tf_op jit(solution)/shard_map/dot_general | solution.py:381
  154.4 3.9 %copy.9 = bf16[1,2048,512]{2,1,0:T(8,128)(2,1)} copy(bf16[1,2048,512]{1,2,0:T(8,128)(2,1)} %fusion) | data formatting | bytes 4194304
  158.3 0.0 copy-start.1
  158.3 4.3 %fusion.1 = bf16[1,512,2048]{2,1,0:T(8,128)(2,1)} fusion(bf16[512,512]{1,0:T(8,128)(2,1)S(1)} %get-tuple-element.8, bf16[512,2048]{1,0:T(8,128)(2,1)} %gather_rows.1), kind=kOutput, calls=%fused_computation.7 | convolution fusion | flops 1075838976 | bytes 4718592 | tf_op jit(solution)/shard_map/dot_general | solution.py:370
  162.7 0.0 copy-done.1
  162.7 0.4 convert_reduce_fusion
  163.1 0.6 dynamic-slice_multiply_fusion
  (2 shorter events, 0.0 us)
Async XLA Ops:
  0.6 53.8 %copy-start = (bf16[1,512,2048]{2,1,0:T(8,128)(2,1)S(1)}, bf16[1,512,2048]{2,1,0:T(8,128)(2,1)}, u32[]{:S(2)}) copy-start(bf16[1,512,2048]{2,1,0:T(8,128)(2,1)} %param.8) | copy-start | bytes 6291460
  34.8 17.5 %copy-start.4 = (f32[512]{0:T(512)S(1)}, f32[512]{0:T(512)}, u32[]{:S(2)}) copy-start(f32[512]{0:T(512)} %param.7) | copy-start | bytes 6148
  39.1 15.0 %copy-start.5 = (bf16[1,256]{1,0:T(2,128)(2,1)S(1)}, bf16[1,256]{1,0:T(2,128)(2,1)}, u32[]{:S(2)}) copy-start(bf16[1,256]{1,0:T(2,128)(2,1)} %param.9) | copy-start | bytes 1540
  132.8 15.8 %copy-start.2 = (bf16[2,256,512]{2,1,0:T(8,128)(2,1)S(1)}, bf16[2,256,512]{2,1,0:T(8,128)(2,1)}, u32[]{:S(2)}) copy-start(bf16[2,256,512]{2,1,0:T(8,128)(2,1)} %layer_sum.2) | copy-start | bytes 1572868
  148.7 3.1 %copy-start.3 = (bf16[512,2048]{1,0:T(8,128)(2,1)S(1)}, bf16[512,2048]{1,0:T(8,128)(2,1)}, u32[]{:S(2)}) copy-start(bf16[512,2048]{1,0:T(8,128)(2,1)} %gather_columns.1) | copy-start | bytes 6291460
  158.3 4.3 %copy-start.1 = (bf16[512,2048]{1,0:T(8,128)(2,1)S(1)}, bf16[512,2048]{1,0:T(8,128)(2,1)}, u32[]{:S(2)}) copy-start(bf16[512,2048]{1,0:T(8,128)(2,1)} %gather_rows.1) | copy-start | bytes 6291460
